TPU v7x, 32 devices: a whole 2x2x4 slice. The times are simulated.
32 devices in a mesh: dp: 4 (over z), head: 8 (over y, x, core).
Axes of the slice: x: 2, y: 2, z: 4, core: 2. Of those that a mesh axis runs over, the one named last changes fastest.
Arguments:
- tokens: bfloat16 [6144, 1152], P('dp'), may hold values from -6 to 6
- seg_ids: int32 [4, 1536], P('dp'), may hold values from 0 to 2, as said below
- time_steps: int32 [12], P('dp'), may hold values from 0 to 999
- head_masks: int32 [12, 16], P('dp', 'head'), may hold values 0 or 1
- skip_masks: int32 [4, 1536], P('dp'), may hold values 0 or 1
- ada_weight: bfloat16 [1152, 6912], P(None, 'head'), may hold values from -0.1875 to 0.1875
- ada_bias: bfloat16 [6912], P('head'), may hold values from -3 to 3
- qkv_weight: bfloat16 [1152, 3, 1152], P(None, None, 'head'), may hold values from -0.1875 to 0.1875
- qv_bias: bfloat16 [2, 1152], P(None, 'head'), may hold values from -2 to 2
- proj_weight: bfloat16 [1152, 1152], P('head'), may hold values from -3 to 3
- proj_bias: bfloat16 [1152], replicated, may hold values from -2 to 2
- fc1_weight: bfloat16 [1152, 4608], P(None, 'head'), may hold values from -0.1875 to 0.1875
- fc1_bias: bfloat16 [4608], P('head'), may hold values from -2 to 2
- fc2_weight: bfloat16 [4608, 1152], P('head'), may hold values from -0.09375 to 0.09375
- fc2_bias: bfloat16 [1152], replicated, may hold values from -2 to 2
- out_cotangent: bfloat16 [6144, 1152], P('dp'), may hold values from -6 to 6
Outputs:
- layer_out: bfloat16 [6144, 1152], P(('dp', 'head'))
- input_grad: float32 [6144, 1152], P(('dp', 'head'))
- ada_weight_grad: float32 [1152, 6912], P(None, 'head')
- ada_bias_grad: float32 [6912], P('head')
- qkv_weight_grad: float32 [1152, 3, 1152], P(None, None, 'head')
- qv_bias_grad: float32 [2, 1152], P(None, 'head')
- proj_weight_grad: float32 [1152, 1152], P('head')
- proj_bias_grad: float32 [1152], replicated
- fc1_weight_grad: float32 [1152, 4608], P(None, 'head')
- fc1_bias_grad: float32 [4608], P('head')
- fc2_weight_grad: float32 [4608, 1152], P('head')
- fc2_bias_grad: float32 [1152], replicated
Inputs may be any that keep to these rules, and one draw needn't show every extreme that they name: `seg_ids`: each pack holds one image of 1024 tokens and two images of 256 tokens, each on neighbouring positions, in an order that the draw chooses for each pack; the image numbers 0, 1, 2 never fall along a pack.
All inputs are finite; a program needn't handle non-finite values. No bound on the sum of `head_masks` or of `skip_masks` on one device may be relied on, other than what follows from the above.
Results may differ from a plain program's by a relative error of at most 0.01255.
The roundings to bfloat16 on the way count: a program that leaves them out, or rounds other values in their place, can miss the bound.
Values may be sent and summed in bfloat16 or wider, within the bound.
A program may use at most 192 MiB of HBM per device.

v0:
```python
import math
import jax
import jax.numpy as jnp
from jax import lax
from jax.sharding import PartitionSpec as P

HEAD_DIM = 72
highest = lax.Precision.HIGHEST


def embed_steps(steps, model_width):
    half_width = model_width // 2
    freqs = jnp.exp(-math.log(10000.0) * jnp.arange(half_width, dtype=jnp.float32) / half_width)
    angles = steps.astype(jnp.float32)[:, None] * freqs[None, :]
    return jnp.concatenate([jnp.cos(angles), jnp.sin(angles)], axis=1)


def normalize(value):
    center = value - jnp.mean(value, axis=-1, keepdims=True)
    return center * lax.rsqrt(jnp.mean(center * center, axis=-1, keepdims=True) + 1e-06)


def norm_back(value, grad):
    return jax.vjp(normalize, value)[1](grad)[0]


def gelu_tanh(value):
    return jax.nn.gelu(value, approximate=True)


def per_token(select, table):
    return jnp.dot(select, table, precision=highest)


def item_sums(select, values):
    return jnp.einsum("sg,sd->gd", select, values, precision=highest)


def attend_forward(queries, key_rows, value_rows, segment, heads_here, score_scale, block_rows):
    length = queries.shape[0]
    q_heads = queries.reshape(length, heads_here, -1)
    k_heads = key_rows.reshape(length, heads_here, -1)
    v_heads = value_rows.reshape(length, heads_here, -1)

    def one_block(start):
        q_block = lax.dynamic_slice_in_dim(q_heads, start, block_rows, 0)
        seg_query = lax.dynamic_slice_in_dim(segment, start, block_rows, 0)
        scores = (
            jnp.einsum("qhe,khe->hqk", q_block, k_heads, preferred_element_type=jnp.float32)
            * score_scale
        )
        scores = jnp.where((seg_query[:, None] == segment[None, :])[None], scores, -1e30)
        row_peak = jnp.max(scores, axis=-1, keepdims=True)
        row_exp = jnp.exp(scores - row_peak)
        row_total = jnp.sum(row_exp, axis=-1, keepdims=True)
        prob_low = (row_exp / row_total).astype(jnp.bfloat16)
        out_block = jnp.einsum(
            "hqk,khe->qhe", prob_low, v_heads, preferred_element_type=jnp.float32
        )
        return (out_block.reshape(block_rows, -1), (row_peak + jnp.log(row_total))[..., 0])

    starts = jnp.arange(length // block_rows, dtype=jnp.int32) * block_rows
    out_blocks, log_totals = lax.map(one_block, starts)
    return (out_blocks.reshape(length, -1), log_totals)


def attend_backward(
    queries,
    key_rows,
    value_rows,
    grad_attn,
    segment,
    log_totals,
    heads_here,
    score_scale,
    block_rows,
):
    length = queries.shape[0]
    q_heads = queries.reshape(length, heads_here, -1)
    k_heads = key_rows.reshape(length, heads_here, -1)
    v_heads = value_rows.reshape(length, heads_here, -1)
    g_heads = grad_attn.reshape(length, heads_here, -1)

    def one_block(carry, inputs):
        start, lse_block = inputs
        grad_keys_acc, grad_values_acc = carry
        q_block = lax.dynamic_slice_in_dim(q_heads, start, block_rows, 0)
        g_block = lax.dynamic_slice_in_dim(g_heads, start, block_rows, 0)
        seg_query = lax.dynamic_slice_in_dim(segment, start, block_rows, 0)
        scores = (
            jnp.einsum("qhe,khe->hqk", q_block, k_heads, preferred_element_type=jnp.float32)
            * score_scale
        )
        scores = jnp.where((seg_query[:, None] == segment[None, :])[None], scores, -1e30)
        probs = jnp.exp(scores - lse_block[..., None])
        grad_probs = jnp.einsum(
            "qhe,khe->hqk", g_block, v_heads, preferred_element_type=jnp.float32
        )
        row_delta = jnp.sum(grad_probs * probs, axis=-1, keepdims=True)
        grad_scores = (probs * (grad_probs - row_delta)).astype(jnp.bfloat16)
        grad_query = (
            jnp.einsum("hqk,khe->qhe", grad_scores, k_heads, preferred_element_type=jnp.float32)
            * score_scale
        )
        grad_keys_acc = grad_keys_acc + jnp.einsum(
            "hqk,qhe->khe", grad_scores, q_block, preferred_element_type=jnp.float32
        )
        grad_values_acc = grad_values_acc + jnp.einsum(
            "hqk,qhe->khe", probs.astype(jnp.bfloat16), g_block, preferred_element_type=jnp.float32
        )
        return (
            (grad_keys_acc, grad_values_acc),
            grad_query.astype(jnp.bfloat16).reshape(block_rows, -1),
        )

    starts = jnp.arange(length // block_rows, dtype=jnp.int32) * block_rows
    zeros_acc = jnp.zeros(k_heads.shape, jnp.float32)
    (grad_keys_acc, grad_values_acc), grad_query = lax.scan(
        one_block, (zeros_acc, zeros_acc), (starts, log_totals)
    )
    grad_keys = (grad_keys_acc * score_scale).astype(jnp.bfloat16).reshape(length, -1)
    grad_values = grad_values_acc.astype(jnp.bfloat16).reshape(length, -1)
    return (grad_query.reshape(length, -1), grad_keys, grad_values)


def local(
    tokens,
    seg_ids,
    time_steps,
    head_masks,
    skip_masks,
    ada_weight,
    ada_bias,
    qkv_weight,
    qv_bias,
    proj_weight,
    proj_bias,
    fc1_weight,
    fc1_bias,
    fc2_weight,
    fc2_bias,
    out_cotangent,
):
    length, model_width = tokens.shape
    groups = time_steps.shape[0]
    heads_here = qkv_weight.shape[2] // HEAD_DIM
    score_scale = HEAD_DIM ** (-0.5)
    block_rows = min(512, length)
    share_rows = length // lax.axis_size("head")
    row_start = lax.axis_index("head") * share_rows
    segment = seg_ids[0]
    keep_tok = skip_masks[0].astype(jnp.float32)[:, None]
    select = (segment[:, None] == jnp.arange(groups, dtype=jnp.int32)[None, :]).astype(jnp.float32)

    def own_rows(value):
        return lax.dynamic_slice_in_dim(value, row_start, share_rows, 0)

    time_act = jax.nn.silu(embed_steps(time_steps, model_width)).astype(jnp.bfloat16)
    mod_part = jnp.dot(time_act, ada_weight, preferred_element_type=jnp.float32) + ada_bias.astype(
        jnp.float32
    )
    modulation = lax.all_gather(mod_part, "head", axis=1, tiled=True)
    shift_one, scale_one = [
        per_token(select, modulation[:, k * model_width : (k + 1) * model_width]) for k in (0, 1)
    ]
    x_full = tokens.astype(jnp.float32)
    norm_one = normalize(x_full)
    h_one = (norm_one * (1.0 + scale_one) + shift_one).astype(jnp.bfloat16)
    proj_three = jnp.einsum("sd,dcj->csj", h_one, qkv_weight, preferred_element_type=jnp.float32)
    qv_float = qv_bias.astype(jnp.float32)
    queries = (proj_three[0] + qv_float[0]).astype(jnp.bfloat16)
    key_rows = proj_three[1].astype(jnp.bfloat16)
    value_rows = (proj_three[2] + qv_float[1]).astype(jnp.bfloat16)
    attended, log_totals = attend_forward(
        queries, key_rows, value_rows, segment, heads_here, score_scale, block_rows
    )
    head_keep = jnp.repeat(per_token(select, head_masks.astype(jnp.float32)), HEAD_DIM, axis=1)
    attn_low = (attended * head_keep).astype(jnp.bfloat16)
    proj_b = proj_bias.astype(jnp.float32)
    fc1_b = fc1_bias.astype(jnp.float32)
    fc2_b = fc2_bias.astype(jnp.float32)

    def scatter_sum(part):
        return lax.psum_scatter(
            part.astype(jnp.bfloat16), "head", scatter_dimension=0, tiled=True
        ).astype(jnp.float32)

    def share_rows_of(value):
        return lax.all_gather(value, "head", axis=0, tiled=True)

    attn_part = jnp.dot(attn_low, proj_weight, preferred_element_type=jnp.float32)
    branch_a = scatter_sum(attn_part) + proj_b
    x_own = own_rows(tokens).astype(jnp.float32)
    select_own = own_rows(select)
    keep_own = own_rows(keep_tok)
    cot_own = own_rows(out_cotangent).astype(jnp.float32)
    shift_one_o, scale_one_o, gate_one_o, shift_two_o, scale_two_o, gate_two_o = jnp.split(
        per_token(select_own, modulation), 6, axis=1
    )
    mid_rows = x_own + gate_one_o * branch_a
    norm_two = normalize(mid_rows)
    h_two = share_rows_of((norm_two * (1.0 + scale_two_o) + shift_two_o).astype(jnp.bfloat16))
    hidden = jnp.dot(h_two, fc1_weight, preferred_element_type=jnp.float32) + fc1_b
    gelu_out = gelu_tanh(hidden).astype(jnp.bfloat16)
    mlp_part = jnp.dot(gelu_out, fc2_weight, preferred_element_type=jnp.float32)
    gate_two = per_token(select, modulation[:, 5 * model_width :])
    grad_m = (out_cotangent.astype(jnp.float32) * gate_two * keep_tok).astype(jnp.bfloat16)
    grad_gelu = jnp.einsum("sd,fd->sf", grad_m, fc2_weight, preferred_element_type=jnp.float32)
    grad_hidden = jax.vjp(gelu_tanh, hidden)[1](grad_gelu)[0].astype(jnp.bfloat16)
    h_two_part = jnp.einsum(
        "sf,df->sd", grad_hidden, fc1_weight, preferred_element_type=jnp.float32
    )
    grad_h_two = scatter_sum(h_two_part)
    fc2_grad = jnp.einsum("sf,sd->fd", gelu_out, grad_m, preferred_element_type=jnp.float32)
    fc2_bias_grad = jnp.sum(grad_m.astype(jnp.float32), axis=0)
    fc1_grad = jnp.einsum("sd,sf->df", h_two, grad_hidden, preferred_element_type=jnp.float32)
    fc1_bias_grad = jnp.sum(grad_hidden.astype(jnp.float32), axis=0)
    branch_m = scatter_sum(mlp_part) + fc2_b
    layer_out = (mid_rows + gate_two_o * keep_own * branch_m).astype(jnp.bfloat16)
    gate_two_grad = item_sums(select_own, cot_own * keep_own * branch_m)
    grad_mid = cot_own + norm_back(mid_rows, grad_h_two * (1.0 + scale_two_o))
    shift_two_grad = item_sums(select_own, grad_h_two)
    scale_two_grad = item_sums(select_own, grad_h_two * norm_two)
    gate_one_grad = item_sums(select_own, grad_mid * branch_a)
    grad_a = share_rows_of((grad_mid * gate_one_o).astype(jnp.bfloat16))
    proj_bias_grad = jnp.sum(grad_a.astype(jnp.float32), axis=0)
    proj_grad = jnp.einsum("sj,sd->jd", attn_low, grad_a, preferred_element_type=jnp.float32)
    grad_attn_low = jnp.einsum(
        "sd,jd->sj", grad_a, proj_weight, preferred_element_type=jnp.float32
    ).astype(jnp.bfloat16)
    grad_attn = grad_attn_low * head_keep.astype(jnp.bfloat16)
    grad_queries, grad_keys, grad_values = attend_backward(
        queries,
        key_rows,
        value_rows,
        grad_attn,
        segment,
        log_totals,
        heads_here,
        score_scale,
        block_rows,
    )
    grad_three = jnp.stack([grad_queries, grad_keys, grad_values])
    qkv_grad = jnp.einsum("sd,csj->dcj", h_one, grad_three, preferred_element_type=jnp.float32)
    qv_bias_grad = jnp.stack(
        [
            jnp.sum(grad_queries.astype(jnp.float32), axis=0),
            jnp.sum(grad_values.astype(jnp.float32), axis=0),
        ]
    )
    h_one_part = jnp.einsum(
        "csj,dcj->sd", grad_three, qkv_weight, preferred_element_type=jnp.float32
    )
    grad_h_one = scatter_sum(h_one_part)
    input_grad = grad_mid + norm_back(x_own, grad_h_one * (1.0 + scale_one_o))
    shift_one_grad = item_sums(select_own, grad_h_one)
    scale_one_grad = item_sums(select_own, grad_h_one * normalize(x_own))
    mod_grad = jnp.concatenate(
        [
            shift_one_grad,
            scale_one_grad,
            gate_one_grad,
            shift_two_grad,
            scale_two_grad,
            gate_two_grad,
        ],
        axis=1,
    )
    mod_cols = lax.psum_scatter(mod_grad, "head", scatter_dimension=1, tiled=True)
    all_cols = lax.all_gather(mod_cols, "dp", axis=0, tiled=True)
    all_act = lax.all_gather(time_act, "dp", axis=0, tiled=True)
    ada_grad = jnp.einsum("gd,gc->dc", all_act.astype(jnp.float32), all_cols, precision=highest)
    ada_bias_grad = jnp.sum(all_cols, axis=0)
    summed = lax.psum(
        (
            qkv_grad.astype(jnp.bfloat16),
            proj_grad.astype(jnp.bfloat16),
            fc1_grad.astype(jnp.bfloat16),
            fc2_grad.astype(jnp.bfloat16),
        ),
        "dp",
    )
    qkv_grad, proj_grad, fc1_grad, fc2_grad = [g.astype(jnp.float32) for g in summed]
    qv_bias_grad, proj_bias_grad, fc1_bias_grad, fc2_bias_grad = lax.psum(
        (qv_bias_grad, proj_bias_grad, fc1_bias_grad, fc2_bias_grad), "dp"
    )
    return (
        layer_out,
        input_grad,
        ada_grad,
        ada_bias_grad,
        qkv_grad,
        qv_bias_grad,
        proj_grad,
        proj_bias_grad,
        fc1_grad,
        fc1_bias_grad,
        fc2_grad,
        fc2_bias_grad,
    )


def solution(mesh):
    placed = (
        P("dp", None),
        P("dp", None),
        P("dp"),
        P("dp", "head"),
        P("dp", None),
        P(None, "head"),
        P("head"),
        P(None, None, "head"),
        P(None, "head"),
        P("head", None),
        P(),
        P(None, "head"),
        P("head"),
        P("head", None),
        P(),
        P("dp", None),
    )
    return jax.shard_map(
        local,
        mesh=mesh,
        in_specs=placed,
        out_specs=(
            P(("dp", "head"), None),
            P(("dp", "head"), None),
            P(None, "head"),
            P("head"),
            P(None, None, "head"),
            P(None, "head"),
            P("head", None),
            P(),
            P(None, "head"),
            P("head"),
            P("head", None),
            P(),
        ),
        check_vma=False,
    )
```

profile of v0, /device:TPU:0, one launch (start us, length us, event | category | flops | bytes accessed | tf_op | source)
XLA Modules:
  0.0 679.6 jit_solution(17424533891599629888)
XLA Ops:
  14.4 10.9 %all-gather = f32[8,864,3]{1,2,0:T(4,128)S(1)} all-gather(f32[1,864,3]{1,2,0:T(4,128)S(1)} %fusion.47), channel_id=1, replica_groups=mesh['dp'=4,'head'=8] {'head'}, dimensions={0}, use_global_device_ids=true | all-gather | bytes 93312 | tf_op jit(solution)/shard_map/all_gather | solution.py:162
  25.5 6.0 fusion.28
  31.5 3.7 fusion.33
  40.1 43.2 %while.27 = (s32[]{:T(128)}, f32[3,512,144]{1,0,2:T(4,128)S(1)}, f32[3,2,512]{2,1,0:T(2,128)S(1)}, s32[3]{0:T(128)S(1)}, s32[1536]{0:T(1024)S(1)}, /*index=5*/s3...) while((s32[]{:T(128)}, f32[3,512,144]{1,0,2:T(4,128)S(1)}, ...), condition=%wide.region_5.6_spmd, body=%wide.region_2.5_spmd.sunk | while | flops 472644608 | bytes 24584384 | solution.py:63
  48.1 3.2 fusion.152
  62.5 3.2 fusion.152
  76.8 3.2 fusion.152
  87.7 4.5 fusion.84
  92.3 43.7 %reduce-scatter.8.cloned.1.call-done = bf16[192,1152]{1,0:T(8,128)(2,1)} async-done(((bf16[1536,1152]{1,0:T(8,128)(2,1)}), bf16[192,1152]{1,0:T(8,128)(2,1)}) %reduce-scatter.8.cloned.1.call-update) | async-done | bytes 442384 | tf_op jit(solution)/shard_map/reduce_scatter | solution.py:184
  140.5 6.0 convert_reduce_fusion.1
  148.3 4.3 fusion.91
  152.6 22.0 %all-gather.6.cloned.1.call-done = bf16[1536,1152]{1,0:T(8,128)(2,1)} async-done(((bf16[192,1152]{1,0:T(8,128)(2,1)}), bf16[1536,1152]{1,0:T(8,128)(2,1)}) %all-gather.6.cloned.1.call-update) | async-done | bytes 3538960 | tf_op jit(solution)/shard_map/all_gather | solution.py:189
  174.5 8.7 %convert_reduce_fusion.3 = (f32[576]{0:T(1024)S(1)}, bf16[1536,576]{0,1:T(8,128)(2,1)S(1)}, f32[1536,576]{0,1:T(8,128)}) fusion(f32[1536,576]{0,1:T(8,128)} %fusion.91, f32[576]{0:T(1024)S(1)} %convert_element_type.194, bf16[1536,1152]{1,0:T(8,128)(2,1)} %all-gather.6.cloned.1.call-done, bf16[1152,576]{0,1:T(8,128)(2,1)S(1)} %copy-done.33), kind=kOutput, calls=%fused_computation.64 | convolution fusion | flops 2058780160 | bytes 13718016 | tf_op jit(solution)/shard_map/dot_general | solution.py:203
  184.4 4.6 convolution_convert_fusion.1
  190.4 7.3 %convolution_convert_fusion.2 = bf16[1536,1152]{1,0:T(8,128)(2,1)} fusion(bf16[576,1152]{1,0:T(8,128)(2,1)S(1)} %copy-done.35, f32[1536,576]{0,1:T(8,128)} %get-tuple-element.244), kind=kOutput, calls=%fused_computation.50 | convolution fusion | flops 2048163840 | bytes 8404992 | tf_op jit(solution)/shard_map/dot_general | solution.py:205
  198.5 38.9 %reduce-scatter.12.cloned.1.call-done = bf16[192,1152]{1,0:T(8,128)(2,1)} async-done(((bf16[1536,1152]{1,0:T(8,128)(2,1)}), bf16[192,1152]{1,0:T(8,128)(2,1)}) %reduce-scatter.12.cloned.1.call-update) | async-done | bytes 442384 | tf_op jit(solution)/shard_map/reduce_scatter | solution.py:184
  238.9 49.9 %reduce-scatter.10.cloned.1.call-done = bf16[192,1152]{1,0:T(8,128)(2,1)} async-done(((bf16[1536,1152]{1,0:T(8,128)(2,1)}), bf16[192,1152]{1,0:T(8,128)(2,1)}) %reduce-scatter.10.cloned.1.call-update) | async-done | bytes 442384 | tf_op jit(solution)/shard_map/reduce_scatter | solution.py:184
  294.4 6.2 convolution_convert_fusion.3
  300.7 4.2 convolution_convert_fusion.4
  304.8 23.6 %all-gather.8.cloned.1.call-done = bf16[1536,1152]{1,0:T(8,128)(2,1)} async-done(((bf16[192,1152]{1,0:T(8,128)(2,1)}), bf16[1536,1152]{1,0:T(8,128)(2,1)}) %all-gather.8.cloned.1.call-update) | async-done | bytes 3538960 | tf_op jit(solution)/shard_map/all_gather | solution.py:189
  328.4 4.1 fusion.42
  332.5 47.8 %while.28 = (s32[]{:T(128)}, f32[1536,2,72]{0,2,1:T(8,128)}, f32[1536,2,72]{0,2,1:T(8,128)S(1)}, bf16[3,512,144]{1,2,0:T(8,128)(2,1)}, s32[3]{0:T(128)S(1)}, /*i...) while((s32[]{:T(128)}, f32[1536,2,72]{0,2,1:T(8,128)}, ...), condition=%wide.region_15.16_spmd.clone, body=%wide.region_13.15_spmd.clone.sunk | while | flops 1148435456 | bytes 61780260 | solution.py:118
  335.8 3.1 subtract_exponential_fusion.3
  351.7 3.1 subtract_exponential_fusion.3
  391.2 4.0 fusion.31
  396.1 13.6 %all-gather.1 = bf16[4,3,1152]{2,1,0:T(4,128)(2,1)S(1)} all-gather(bf16[1,3,1152]{2,1,0:T(4,128)(2,1)S(1)} %fusion.129), channel_id=1, replica_groups=mesh['dp'=4,'head'=8] {'dp'}, dimensions={0}, use_global_device_ids=true | all-gather | bytes 34560 | tf_op jit(solution)/shard_map/all_gather | solution.py:271
  412.5 21.6 %all-reduce = (f32[2,144]{1,0:T(2,128)}, f32[1152]{0:T(1024)}, f32[576]{0:T(1024)}, f32[1152]{0:T(1024)}) all-reduce(f32[2,144]{1,0:T(2,128)S(1)} %pad_maximum_fusion.2, f32[1152]{0:T(1024)S(1)} %convert_reduce_fusion.2, f32[576]{0:T(1024)S(1)} %get-tuple-element.222, ...), channel_id=1, replica_groups=mesh['dp'=4,'head'=8] {'dp'}, use_global_device_ids=true, to_apply=%region_26.27 | all-reduce | flops 3168 | bytes 25344 | tf_op jit(solution)/shard_map/psum | solution.py:284
  434.2 106.8 %all-reduce.4.cloned.1.call-done = (bf16[1152,3,144]{0,2,1:T(8,128)(2,1)}, bf16[144,1152]{1,0:T(8,128)(2,1)}, bf16[1152,576]{0,1:T(8,128)(2,1)}, bf16[576,1152]{1,0:T(8,128)(2,1)}) async-done(((bf16[1152,3,144]{0,2,1:T(8,128)(2,1)}, bf16[144,1152]{1,0:T(8,128)(2,1)}, bf16[1152,576]{0,1:T(8,128)(2,1)}, bf16[576,1152]{1,0:T(8,128)(2,1)}), (bf16[1152,3,144]{0,2,1:T(8,128)(2,1)}, bf16[144,1152]{1,0:T(8,128)(2,1)}, ...) | async-done | bytes 3981328 | tf_op jit(solution)/shard_map/psum | solution.py:274
  549.1 43.5 %reduce-scatter.14.cloned.1.call-done = bf16[192,1152]{1,0:T(8,128)(2,1)} async-done(((bf16[1536,1152]{1,0:T(8,128)(2,1)}), bf16[192,1152]{1,0:T(8,128)(2,1)}) %reduce-scatter.14.cloned.1.call-update) | async-done | bytes 442384 | tf_op jit(solution)/shard_map/reduce_scatter | solution.py:184
  608.3 45.6 %reduce-scatter.16.cloned.1.call-done = f32[864,3]{1,0:T(8,128)} async-done(((f32[6912,3]{1,0:T(8,128)}), f32[864,3]{1,0:T(8,128)}) %reduce-scatter.16.cloned.1.call-update) | async-done | bytes 10384
  655.1 13.1 %all-gather.2 = f32[4,3,864]{2,1,0:T(4,128)S(1)} all-gather(f32[1,3,864]{2,1,0:T(4,128)S(1)} %bitcast.149), channel_id=1, replica_groups=mesh['dp'=4,'head'=8] {'dp'}, dimensions={0}, use_global_device_ids=true | all-gather | bytes 51840 | tf_op jit(solution)/shard_map/all_gather | solution.py:270
  668.9 3.7 fusion.92
  (253 shorter events, 136.2 us)
Async XLA Ops:
  7.2 6.6 copy-start
  7.2 128.7 %reduce-scatter.8.cloned.1.call-start = ((), (), s32[]{:S(2)}) async-start(), calls=%async_computation.5 | async-start | bytes 3981312 | tf_op jit(solution)/shard_map/reduce_scatter | solution.py:184
  13.8 17.7 %copy-start.24 = (f32[3,576]{1,0:T(4,128)}, f32[3,576]{1,0:T(4,128)S(1)}, u32[]{:S(2)}) copy-start(f32[3,576]{1,0:T(4,128)S(1)} %get-tuple-element.240) | copy-start | bytes 20740
  13.8 17.7 %copy-start.26 = (f32[3,576]{1,0:T(4,128)}, f32[3,576]{1,0:T(4,128)S(1)}, u32[]{:S(2)}) copy-start(f32[3,576]{1,0:T(4,128)S(1)} %get-tuple-element.241) | copy-start | bytes 20740
  31.5 3.8 copy-start.36
  84.3 3.1 copy-start.9
  84.3 3.1 copy-start.29
  87.4 87.2 %all-gather.6.cloned.1.call-start = ((), (), s32[]{:S(2)}) async-start(), calls=%async_computation.6 | async-start | bytes 3981312 | tf_op jit(solution)/shard_map/all_gather | solution.py:189
  87.7 4.5 copy-start.19
  92.3 48.2 %copy-start.31 = (bf16[576]{0:T(1024)(128)(2,1)S(1)}, bf16[576]{0:T(1024)(128)(2,1)}, u32[]{:S(2)}) copy-start(bf16[576]{0:T(1024)(128)(2,1)} %param.32) | copy-start | bytes 3460
  92.3 48.2 %copy-start.28 = (s32[1,1536]{1,0:T(1,128)S(1)}, s32[1,1536]{1,0:T(1,128)}, u32[]{:S(2)}) copy-start(s32[1,1536]{1,0:T(1,128)} %param.24) | copy-start | bytes 18436
  140.4 96.9 %reduce-scatter.12.cloned.1.call-start = ((), (), s32[]{:S(2)}) async-start(), calls=%async_computation.8 | async-start | bytes 3981312 | tf_op jit(solution)/shard_map/reduce_scatter | solution.py:184
  140.5 7.8 %copy-start.34 = (bf16[576,1152]{1,0:T(8,128)(2,1)S(1)}, bf16[576,1152]{1,0:T(8,128)(2,1)}, u32[]{:S(2)}) copy-start(bf16[576,1152]{1,0:T(8,128)(2,1)} %param.33) | copy-start | bytes 3981316
  148.3 26.2 %copy-start.33 = (bf16[1152,576]{0,1:T(8,128)(2,1)S(1)}, bf16[1152,576]{0,1:T(8,128)(2,1)}, u32[]{:S(2)}) copy-start(bf16[1152,576]{0,1:T(8,128)(2,1)} %param.31) | copy-start | bytes 3981316
  189.1 99.7 %reduce-scatter.10.cloned.1.call-start = ((), (), s32[]{:S(2)}) async-start(), calls=%async_computation.7 | async-start | bytes 3981312 | tf_op jit(solution)/shard_map/reduce_scatter | solution.py:184
  197.7 130.7 %all-gather.8.cloned.1.call-start = ((), (), s32[]{:S(2)}) async-start(), calls=%async_computation.9 | async-start | bytes 3981312 | tf_op jit(solution)/shard_map/all_gather | solution.py:189
  294.3 246.7 %all-reduce.4.cloned.1.call-start = ((), (), s32[]{:S(2)}) async-start(), calls=%async_computation.12 | async-start | bytes 7962624 | tf_op jit(solution)/shard_map/psum | solution.py:274
  294.4 6.2 copy-start.40
  294.4 6.2 copy-start.41
  300.6 27.8 %copy-start.23 = (bf16[144,1152]{1,0:T(8,128)(2,1)S(1)}, bf16[144,1152]{1,0:T(8,128)(2,1)}, u32[]{:S(2)}) copy-start(bf16[144,1152]{1,0:T(8,128)(2,1)} %param.29) | copy-start | bytes 995332
  390.0 202.5 %reduce-scatter.14.cloned.1.call-start = ((), (), s32[]{:S(2)}) async-start(), calls=%async_computation.10 | async-start | bytes 3981312 | tf_op jit(solution)/shard_map/reduce_scatter | solution.py:184
  395.3 14.5 %copy-start.15 = (bf16[3,512,144]{1,2,0:T(8,128)(2,1)S(1)}, bf16[3,512,144]{1,2,0:T(8,128)(2,1)}, u32[]{:S(2)}) copy-start(bf16[3,512,144]{1,2,0:T(8,128)(2,1)} %get-tuple-element.126) | copy-start | bytes 1327108
  395.3 258.6 %reduce-scatter.16.cloned.1.call-start = ((), (), s32[]{:S(2)}) async-start(), calls=%async_computation.11 | async-start | bytes 3981312
  541.0 4.7 copy-start.17
  543.0 4.4 copy-start.16
  547.4 49.8 %copy-start.20 = (pred[1536,3]{1,0:T(32,128)(4,1)S(1)}, pred[1536,3]{1,0:T(32,128)(4,1)}, u32[]{:S(2)}) copy-start(pred[1536,3]{1,0:T(32,128)(4,1)} %copy-done.19) | copy-start | bytes 13828
  549.1 50.0 %copy-start.7 = (f32[192,1152]{1,0:T(8,128)S(1)}, f32[192,1152]{1,0:T(8,128)}, u32[]{:S(2)}) copy-start(f32[192,1152]{1,0:T(8,128)} %copy-done.6) | copy-start | bytes 2654212
  549.1 50.0 %copy-start.14 = (bf16[192,1152]{1,0:T(8,128)(2,1)S(1)}, bf16[192,1152]{1,0:T(8,128)(2,1)}, u32[]{:S(2)}) copy-start(bf16[192,1152]{1,0:T(8,128)(2,1)} %reduce-scatter.8.cloned.1.call-done) | copy-start | bytes 1327108
  549.1 51.7 %copy-start.8 = (bf16[192,1152]{1,0:T(8,128)(2,1)S(1)}, bf16[192,1152]{1,0:T(8,128)(2,1)}, u32[]{:S(2)}) copy-start(bf16[192,1152]{1,0:T(8,128)(2,1)} %reduce-scatter.12.cloned.1.call-done) | copy-start | bytes 1327108
  592.6 4.6 copy-start.11
  594.5 7.2 %copy-start.21 = (bf16[192,1152]{1,0:T(8,128)(2,1)S(1)}, bf16[192,1152]{1,0:T(8,128)(2,1)}, u32[]{:S(2)}) copy-start(bf16[192,1152]{1,0:T(8,128)(2,1)} %reduce-scatter.10.cloned.1.call-done) | copy-start | bytes 1327108
  605.7 66.9 %copy-start.1 = (bf16[1152,864]{0,1:T(8,128)(2,1)S(1)}, bf16[1152,864]{0,1:T(8,128)(2,1)}, u32[]{:S(2)}) copy-start(bf16[1152,864]{0,1:T(8,128)(2,1)} %param.25) | copy-start | bytes 5971972
  (23 other events, 38.7 us)
Sparse Core Ops, SparseCore 0:
  87.5 48.3 reduce-scatter.7
  140.5 33.9 all-gather.5
  189.2 48.0 reduce-scatter.11
  240.7 48.0 reduce-scatter.9
  294.4 33.9 all-gather.7
  390.2 150.7 all-reduce.3
  545.5 47.0 reduce-scatter.13
  605.8 48.0 reduce-scatter.15
where the time goes:
time: 684 us; the launch traced here: 680 us
  waiting for transfers between devices  374 us (55%)
  matrix products  135 us (20%)
  blocking collectives  59.2 us (9%)
  other arithmetic  51.4 us (8%)
  local copies, waits for them, and re-layouts  32.4 us (5%)
  between operations  14.9 us (2%)
  loops' own time  12.4 us (2%)
    reduce_scatter x4, waiting for transfers between devices, scatter_sum(): lax.psum_scatter(part.astype(jnp.bfloat16), 'head', scatter_dimension=0,...  176 us
    psum x1, waiting for transfers between devices, local(): lax.psum((qkv_grad.astype(jnp.bfloat16), proj_grad.astype(jnp.bfloat16),...  107 us
    unnamed x9, waiting for transfers between devices  45.7 us
    all_gather x2, waiting for transfers between devices, share_rows_of(): return lax.all_gather(value, 'head', axis=0, tiled=True)  45.5 us
    psum x1, blocking collectives, local(): lax.psum((qv_bias_grad, proj_bias_grad, fc1_bias_grad, fc2_bias_grad), 'dp')  21.6 us
    dot_general x5, matrix products, per_token(): return jnp.dot(select, table, precision=highest)  20.8 us
    dot_general x6, matrix products, one_block(): jnp.einsum('qhe,khe->hqk', q_block, k_heads, preferred_element_type=jnp.f...  17.9 us
  transfers between devices with their start and end apart: 8, of which 8 were waited for; matrix products, arithmetic and copies ran while one was open for 8% of the time, Pallas kernels for 0%

commit v1 on v0

--- a/solution.py
+++ b/solution.py
@@ -267,8 +267,13 @@
         axis=1,
     )
     mod_cols = lax.psum_scatter(mod_grad, "head", scatter_dimension=1, tiled=True)
-    all_cols = lax.all_gather(mod_cols, "dp", axis=0, tiled=True)
-    all_act = lax.all_gather(time_act, "dp", axis=0, tiled=True)
+    all_cols, all_act = jnp.split(
+        lax.all_gather(
+            jnp.concatenate([mod_cols, time_act], 1), axis_name="dp", axis=0, tiled=True
+        ),
+        [mod_cols.shape[1]],
+        1,
+    )
     ada_grad = jnp.einsum("gd,gc->dc", all_act.astype(jnp.float32), all_cols, precision=highest)
     ada_bias_grad = jnp.sum(all_cols, axis=0)
     summed = lax.psum(

time: 684 us -> 685 us (level)
  blocking collectives: 59.2 us -> 45 us
  waiting for transfers between devices: 374 us -> 388 us
    psum x1, waiting for transfers between devices: 107 us -> 121 us  [local(): lax.psum((qkv_grad.astype(jnp.bfloat16), proj_grad.astype(jnp.bfloat16),...]
    all_gather x2 -> x1, blocking collectives: 26.7 us -> 13.5 us  [local(): lax.all_gather(jnp.concatenate([mod_cols, time_act], 1), axis_name='dp',...]
where the time goes in v1:
time: 685 us; the launch traced here: 681 us
  waiting for transfers between devices  388 us (57%)
  matrix products  136 us (20%)
  other arithmetic  51.5 us (8%)
  blocking collectives  45 us (7%)
  local copies, waits for them, and re-layouts  32.5 us (5%)
  between operations  14.9 us (2%)
  loops' own time  12.4 us (2%)
    reduce_scatter x4, waiting for transfers between devices, scatter_sum(): lax.psum_scatter(part.astype(jnp.bfloat16), 'head', scatter_dimension=0,...  176 us
    psum x1, waiting for transfers between devices, local(): lax.psum((qkv_grad.astype(jnp.bfloat16), proj_grad.astype(jnp.bfloat16),...  121 us
    unnamed x9, waiting for transfers between devices  45.7 us
    all_gather x2, waiting for transfers between devices, share_rows_of(): return lax.all_gather(value, 'head', axis=0, tiled=True)  45.5 us
    dot_general x5, matrix products, per_token(): return jnp.dot(select, table, precision=highest)  20.8 us
    psum x1, blocking collectives, local(): lax.psum((qv_bias_grad, proj_bias_grad, fc1_bias_grad, fc2_bias_grad), 'dp')  20.7 us
    dot_general x6, matrix products, one_block(): jnp.einsum('qhe,khe->hqk', q_block, k_heads, preferred_element_type=jnp.f...  17.9 us
  transfers between devices with their start and end apart: 8, of which 8 were waited for; matrix products, arithmetic and copies ran while one was open for 8% of the time, Pallas kernels for 0%

profile of v1, /device:TPU:0, one launch (start us, length us, event | category | flops | bytes accessed | tf_op | source)
XLA Modules:
  0.0 681.1 jit_solution(15921227245692752176)
XLA Ops:
  14.4 10.9 %all-gather = f32[8,864,3]{1,2,0:T(4,128)S(1)} all-gather(f32[1,864,3]{1,2,0:T(4,128)S(1)} %fusion.47), channel_id=1, replica_groups=mesh['dp'=4,'head'=8] {'head'}, dimensions={0}, use_global_device_ids=true | all-gather | bytes 93312 | tf_op jit(solution)/shard_map/all_gather | solution.py:162
  25.5 6.0 fusion.28
  31.5 3.7 fusion.33
  40.1 43.2 %while.27 = (s32[]{:T(128)}, f32[3,512,144]{1,0,2:T(4,128)S(1)}, f32[3,2,512]{2,1,0:T(2,128)S(1)}, s32[3]{0:T(128)S(1)}, s32[1536]{0:T(1024)S(1)}, /*index=5*/s3...) while((s32[]{:T(128)}, f32[3,512,144]{1,0,2:T(4,128)S(1)}, ...), condition=%wide.region_5.6_spmd, body=%wide.region_2.5_spmd.sunk | while | flops 472644608 | bytes 24584384 | solution.py:63
  48.1 3.2 fusion.151
  62.5 3.2 fusion.151
  76.8 3.2 fusion.151
  87.7 4.5 fusion.89
  92.3 43.7 %reduce-scatter.8.cloned.1.call-done = bf16[192,1152]{1,0:T(8,128)(2,1)} async-done(((bf16[1536,1152]{1,0:T(8,128)(2,1)}), bf16[192,1152]{1,0:T(8,128)(2,1)}) %reduce-scatter.8.cloned.1.call-update) | async-done | bytes 442384 | tf_op jit(solution)/shard_map/reduce_scatter | solution.py:184
  140.5 6.0 convert_reduce_fusion.1
  148.3 4.3 fusion.96
  152.6 22.0 %all-gather.5.cloned.1.call-done = bf16[1536,1152]{1,0:T(8,128)(2,1)} async-done(((bf16[192,1152]{1,0:T(8,128)(2,1)}), bf16[1536,1152]{1,0:T(8,128)(2,1)}) %all-gather.5.cloned.1.call-update) | async-done | bytes 3538960 | tf_op jit(solution)/shard_map/all_gather | solution.py:189
  174.5 8.7 %convert_reduce_fusion.3 = (f32[576]{0:T(1024)S(1)}, bf16[1536,576]{0,1:T(8,128)(2,1)S(1)}, f32[1536,576]{0,1:T(8,128)}) fusion(f32[1536,576]{0,1:T(8,128)} %fusion.96, f32[576]{0:T(1024)S(1)} %convert_element_type.196, bf16[1536,1152]{1,0:T(8,128)(2,1)} %all-gather.5.cloned.1.call-done, bf16[1152,576]{0,1:T(8,128)(2,1)S(1)} %copy-done.33), kind=kOutput, calls=%fused_computation.64 | convolution fusion | flops 2058780160 | bytes 13718016 | tf_op jit(solution)/shard_map/dot_general | solution.py:203
  184.4 4.6 convolution_convert_fusion.1
  190.4 7.3 %convolution_convert_fusion.2 = bf16[1536,1152]{1,0:T(8,128)(2,1)} fusion(bf16[576,1152]{1,0:T(8,128)(2,1)S(1)} %copy-done.35, f32[1536,576]{0,1:T(8,128)} %get-tuple-element.244), kind=kOutput, calls=%fused_computation.50 | convolution fusion | flops 2048163840 | bytes 8404992 | tf_op jit(solution)/shard_map/dot_general | solution.py:205
  198.5 38.9 %reduce-scatter.12.cloned.1.call-done = bf16[192,1152]{1,0:T(8,128)(2,1)} async-done(((bf16[1536,1152]{1,0:T(8,128)(2,1)}), bf16[192,1152]{1,0:T(8,128)(2,1)}) %reduce-scatter.12.cloned.1.call-update) | async-done | bytes 442384 | tf_op jit(solution)/shard_map/reduce_scatter | solution.py:184
  238.9 49.9 %reduce-scatter.10.cloned.1.call-done = bf16[192,1152]{1,0:T(8,128)(2,1)} async-done(((bf16[1536,1152]{1,0:T(8,128)(2,1)}), bf16[192,1152]{1,0:T(8,128)(2,1)}) %reduce-scatter.10.cloned.1.call-update) | async-done | bytes 442384 | tf_op jit(solution)/shard_map/reduce_scatter | solution.py:184
  294.4 6.2 convolution_convert_fusion.3
  300.7 4.2 convolution_convert_fusion.4
  304.8 23.6 %all-gather.7.cloned.1.call-done = bf16[1536,1152]{1,0:T(8,128)(2,1)} async-done(((bf16[192,1152]{1,0:T(8,128)(2,1)}), bf16[1536,1152]{1,0:T(8,128)(2,1)}) %all-gather.7.cloned.1.call-update) | async-done | bytes 3538960 | tf_op jit(solution)/shard_map/all_gather | solution.py:189
  328.4 4.1 fusion.42
  332.5 47.8 %while.28 = (s32[]{:T(128)}, f32[1536,2,72]{0,2,1:T(8,128)}, f32[1536,2,72]{0,2,1:T(8,128)S(1)}, bf16[3,512,144]{1,2,0:T(8,128)(2,1)}, s32[3]{0:T(128)S(1)}, /*i...) while((s32[]{:T(128)}, f32[1536,2,72]{0,2,1:T(8,128)}, ...), condition=%wide.region_15.16_spmd.clone, body=%wide.region_13.15_spmd.clone.sunk | while | flops 1148435456 | bytes 61780260 | solution.py:118
  335.8 3.1 subtract_exponential_fusion.3
  351.7 3.1 subtract_exponential_fusion.3
  367.6 3.1 subtract_exponential_fusion.3
  391.2 4.0 fusion.31
  399.2 20.7 %all-reduce = (f32[2,144]{1,0:T(2,128)}, f32[1152]{0:T(1024)}, f32[576]{0:T(1024)}, f32[1152]{0:T(1024)}) all-reduce(f32[2,144]{1,0:T(2,128)S(1)} %pad_maximum_fusion.2, f32[1152]{0:T(1024)S(1)} %convert_reduce_fusion.2, f32[576]{0:T(1024)S(1)} %get-tuple-element.222, ...), channel_id=1, replica_groups=mesh['dp'=4,'head'=8] {'dp'}, use_global_device_ids=true, to_apply=%region_26.27 | all-reduce | flops 3168 | bytes 25344 | tf_op jit(solution)/shard_map/psum | solution.py:289
  419.9 120.6 %all-reduce.4.cloned.1.call-done = (bf16[1152,3,144]{0,2,1:T(8,128)(2,1)}, bf16[144,1152]{1,0:T(8,128)(2,1)}, bf16[1152,576]{0,1:T(8,128)(2,1)}, bf16[576,1152]{1,0:T(8,128)(2,1)}) async-done(((bf16[1152,3,144]{0,2,1:T(8,128)(2,1)}, bf16[144,1152]{1,0:T(8,128)(2,1)}, bf16[1152,576]{0,1:T(8,128)(2,1)}, bf16[576,1152]{1,0:T(8,128)(2,1)}), (bf16[1152,3,144]{0,2,1:T(8,128)(2,1)}, bf16[144,1152]{1,0:T(8,128)(2,1)}, ...) | async-done | bytes 3981328 | tf_op jit(solution)/shard_map/psum | solution.py:279
  548.5 43.5 %reduce-scatter.14.cloned.1.call-done = bf16[192,1152]{1,0:T(8,128)(2,1)} async-done(((bf16[1536,1152]{1,0:T(8,128)(2,1)}), bf16[192,1152]{1,0:T(8,128)(2,1)}) %reduce-scatter.14.cloned.1.call-update) | async-done | bytes 442384 | tf_op jit(solution)/shard_map/reduce_scatter | solution.py:184
  607.7 45.6 %reduce-scatter.16.cloned.1.call-done = f32[864,3]{1,0:T(8,128)} async-done(((f32[6912,3]{1,0:T(8,128)}), f32[864,3]{1,0:T(8,128)}) %reduce-scatter.16.cloned.1.call-update) | async-done | bytes 10384
  654.6 13.5 %all-gather.1 = f32[4,3,2016]{2,1,0:T(4,128)S(1)} all-gather(f32[1,3,2016]{2,1,0:T(4,128)S(1)} %maximum_bitcast_fusion), channel_id=1, replica_groups=mesh['dp'=4,'head'=8] {'dp'}, dimensions={0}, use_global_device_ids=true | all-gather | bytes 120960 | tf_op jit(solution)/shard_map/all_gather | solution.py:271
  668.8 5.3 fusion.75
  (252 shorter events, 133.4 us)
Async XLA Ops:
  7.2 6.6 copy-start
  7.2 128.7 %reduce-scatter.8.cloned.1.call-start = ((), (), s32[]{:S(2)}) async-start(), calls=%async_computation.5 | async-start | bytes 3981312 | tf_op jit(solution)/shard_map/reduce_scatter | solution.py:184
  9.5 3.1 copy-start.2
  13.8 17.7 %copy-start.24 = (f32[3,576]{1,0:T(4,128)}, f32[3,576]{1,0:T(4,128)S(1)}, u32[]{:S(2)}) copy-start(f32[3,576]{1,0:T(4,128)S(1)} %get-tuple-element.240) | copy-start | bytes 20740
  13.8 17.7 %copy-start.26 = (f32[3,576]{1,0:T(4,128)}, f32[3,576]{1,0:T(4,128)S(1)}, u32[]{:S(2)}) copy-start(f32[3,576]{1,0:T(4,128)S(1)} %get-tuple-element.241) | copy-start | bytes 20740
  31.5 3.8 copy-start.36
  84.3 3.1 copy-start.9
  84.3 3.1 copy-start.29
  87.4 87.2 %all-gather.5.cloned.1.call-start = ((), (), s32[]{:S(2)}) async-start(), calls=%async_computation.6 | async-start | bytes 3981312 | tf_op jit(solution)/shard_map/all_gather | solution.py:189
  87.7 4.5 copy-start.19
  92.3 48.2 %copy-start.31 = (bf16[576]{0:T(1024)(128)(2,1)S(1)}, bf16[576]{0:T(1024)(128)(2,1)}, u32[]{:S(2)}) copy-start(bf16[576]{0:T(1024)(128)(2,1)} %param.32) | copy-start | bytes 3460
  92.3 48.2 %copy-start.28 = (s32[1,1536]{1,0:T(1,128)S(1)}, s32[1,1536]{1,0:T(1,128)}, u32[]{:S(2)}) copy-start(s32[1,1536]{1,0:T(1,128)} %param.24) | copy-start | bytes 18436
  140.4 96.9 %reduce-scatter.12.cloned.1.call-start = ((), (), s32[]{:S(2)}) async-start(), calls=%async_computation.8 | async-start | bytes 3981312 | tf_op jit(solution)/shard_map/reduce_scatter | solution.py:184
  140.5 7.8 %copy-start.34 = (bf16[576,1152]{1,0:T(8,128)(2,1)S(1)}, bf16[576,1152]{1,0:T(8,128)(2,1)}, u32[]{:S(2)}) copy-start(bf16[576,1152]{1,0:T(8,128)(2,1)} %param.33) | copy-start | bytes 3981316
  148.3 26.2 %copy-start.33 = (bf16[1152,576]{0,1:T(8,128)(2,1)S(1)}, bf16[1152,576]{0,1:T(8,128)(2,1)}, u32[]{:S(2)}) copy-start(bf16[1152,576]{0,1:T(8,128)(2,1)} %param.31) | copy-start | bytes 3981316
  189.1 99.7 %reduce-scatter.10.cloned.1.call-start = ((), (), s32[]{:S(2)}) async-start(), calls=%async_computation.7 | async-start | bytes 3981312 | tf_op jit(solution)/shard_map/reduce_scatter | solution.py:184
  197.7 130.7 %all-gather.7.cloned.1.call-start = ((), (), s32[]{:S(2)}) async-start(), calls=%async_computation.9 | async-start | bytes 3981312 | tf_op jit(solution)/shard_map/all_gather | solution.py:189
  294.3 246.1 %all-reduce.4.cloned.1.call-start = ((), (), s32[]{:S(2)}) async-start(), calls=%async_computation.12 | async-start | bytes 7962624 | tf_op jit(solution)/shard_map/psum | solution.py:279
  294.4 6.2 copy-start.40
  294.4 6.2 copy-start.41
  300.6 27.8 %copy-start.23 = (bf16[144,1152]{1,0:T(8,128)(2,1)S(1)}, bf16[144,1152]{1,0:T(8,128)(2,1)}, u32[]{:S(2)}) copy-start(bf16[144,1152]{1,0:T(8,128)(2,1)} %param.29) | copy-start | bytes 995332
  390.0 202.0 %reduce-scatter.14.cloned.1.call-start = ((), (), s32[]{:S(2)}) async-start(), calls=%async_computation.10 | async-start | bytes 3981312 | tf_op jit(solution)/shard_map/reduce_scatter | solution.py:184
  395.3 258.0 %reduce-scatter.16.cloned.1.call-start = ((), (), s32[]{:S(2)}) async-start(), calls=%async_computation.11 | async-start | bytes 3981312
  540.4 4.7 copy-start.17
  542.4 4.4 copy-start.16
  546.8 49.8 %copy-start.20 = (pred[1536,3]{1,0:T(32,128)(4,1)S(1)}, pred[1536,3]{1,0:T(32,128)(4,1)}, u32[]{:S(2)}) copy-start(pred[1536,3]{1,0:T(32,128)(4,1)} %copy-done.19) | copy-start | bytes 13828
  548.5 50.0 %copy-start.7 = (f32[192,1152]{1,0:T(8,128)S(1)}, f32[192,1152]{1,0:T(8,128)}, u32[]{:S(2)}) copy-start(f32[192,1152]{1,0:T(8,128)} %copy-done.6) | copy-start | bytes 2654212
  548.5 50.0 %copy-start.14 = (bf16[192,1152]{1,0:T(8,128)(2,1)S(1)}, bf16[192,1152]{1,0:T(8,128)(2,1)}, u32[]{:S(2)}) copy-start(bf16[192,1152]{1,0:T(8,128)(2,1)} %reduce-scatter.8.cloned.1.call-done) | copy-start | bytes 1327108
  548.5 51.7 %copy-start.8 = (bf16[192,1152]{1,0:T(8,128)(2,1)S(1)}, bf16[192,1152]{1,0:T(8,128)(2,1)}, u32[]{:S(2)}) copy-start(bf16[192,1152]{1,0:T(8,128)(2,1)} %reduce-scatter.12.cloned.1.call-done) | copy-start | bytes 1327108
  592.0 4.6 copy-start.11
  593.9 7.2 %copy-start.21 = (bf16[192,1152]{1,0:T(8,128)(2,1)S(1)}, bf16[192,1152]{1,0:T(8,128)(2,1)}, u32[]{:S(2)}) copy-start(bf16[192,1152]{1,0:T(8,128)(2,1)} %reduce-scatter.10.cloned.1.call-done) | copy-start | bytes 1327108
  605.1 68.9 %copy-start.1 = (bf16[1152,864]{0,1:T(8,128)(2,1)S(1)}, bf16[1152,864]{0,1:T(8,128)(2,1)}, u32[]{:S(2)}) copy-start(bf16[1152,864]{0,1:T(8,128)(2,1)} %param.25) | copy-start | bytes 5971972
  (23 other events, 36.8 us)
Sparse Core Ops, SparseCore 0:
  87.5 48.3 reduce-scatter.7
  140.5 33.9 all-gather.4
  189.2 48.0 reduce-scatter.11
  240.7 48.0 reduce-scatter.9
  294.4 33.9 all-gather.6
  390.2 150.2 all-reduce.3
  544.9 47.0 reduce-scatter.13
  605.2 48.0 reduce-scatter.15
